TPU v7x, 256 devices: a whole 4x4x8 slice. The times are simulated.
256 devices in a mesh: dp: 32 (over y, x, core), filter: 8 (over z).
Axes of the slice: x: 4, y: 4, z: 8, core: 2. Of those that a mesh axis runs over, the one named last changes fastest.
Arguments:
- inputs: bfloat16 [32, 48, 24, 1024], P('dp', None, None, 'filter'), may hold values from -6 to 6
- kernel: bfloat16 [3, 3, 1024, 1024], P(None, None, 'filter'), may hold values from -0.0625 to 0.0625
- cotangent: bfloat16 [32, 48, 24, 1024], P('dp', 'filter'), may hold values from -6 to 6
Outputs:
- outputs: bfloat16 [32, 48, 24, 1024], P('dp', 'filter')
- input_grad: bfloat16 [32, 48, 24, 1024], P('dp', None, None, 'filter')
- kernel_grad: float32 [1024, 3, 3, 1024], P('dp', None, None, 'filter')
All inputs are finite; a program needn't handle non-finite values.
Results may differ from a plain program's by a relative error of at most 0.001.
Values may be sent and summed in bfloat16 or wider, within the bound.
No kernel may reach another device: no remote copies, remote signals or barrier semaphores. Data moves between devices by JAX's collectives and lax.ppermute only.
A program may use at most 128 MiB of HBM per device.

v0:
```python
import jax
import jax.numpy as jnp
from jax import lax
from jax.sharding import PartitionSpec as P


def conv_rows(xpad, weights, count, width):
    total = jnp.zeros((count, width, weights.shape[3]), jnp.float32)
    for a in range(3):
        for b in range(3):
            total = total + jnp.einsum(
                "hwi,io->hwo",
                xpad[a : a + count, b : b + width],
                weights[a, b],
                preferred_element_type=jnp.float32,
            )
    return total


def on_device(inputs, kernel, cotangent):
    sample = inputs[0]
    height = sample.shape[0]
    width = sample.shape[1]
    local_in = sample.shape[2]
    channels = kernel.shape[3]
    groups = lax.axis_size("filter")
    my_rows = height // groups
    xpad = jnp.pad(sample, ((1, 1), (1, 1), (0, 0)))
    summed = lax.psum_scatter(
        conv_rows(xpad, kernel, my_rows * lax.axis_size("filter"), width),
        "filter",
        scatter_dimension=0,
        tiled=True,
    )
    outputs = summed.astype(jnp.bfloat16)[None]
    start = jnp.int32(0)
    back_pad = jnp.zeros((height + 2, width + 2, local_in), jnp.float32)
    grad_rows = lax.all_gather(cotangent, "filter", axis=1, tiled=True)[0]
    count = grad_rows.shape[0]
    taps = []
    for a in range(3):
        for b in range(3):
            contrib = jnp.einsum(
                "hwo,io->hwi", grad_rows, kernel[a, b], preferred_element_type=jnp.float32
            )
            region = lax.dynamic_slice(back_pad, (start + a, b, 0), (count, width, local_in))
            back_pad = lax.dynamic_update_slice(back_pad, region + contrib, (start + a, b, 0))
            taps.append(
                jnp.einsum(
                    "hwi,hwo->oi",
                    xpad[a : a + count, b : b + width],
                    grad_rows,
                    preferred_element_type=jnp.float32,
                )
            )
    grads = jnp.stack(taps, 1).reshape(channels, 3, 3, local_in)
    back_pad, grads = (back_pad, grads)
    input_grad = back_pad[1:-1, 1:-1].astype(jnp.bfloat16)[None]
    samples = lax.axis_size("dp")
    scale = 1.0 / jnp.sqrt(jnp.float32(samples * height * width))
    whole = lax.psum(grads, "dp")
    share = channels // samples
    mine = lax.dynamic_slice_in_dim(whole, lax.axis_index("dp") * share, share, 0)
    return (outputs, input_grad, mine * scale)


def solution(mesh):
    return jax.shard_map(
        on_device,
        mesh=mesh,
        in_specs=(
            P("dp", None, None, "filter"),
            P(None, None, "filter", None),
            P("dp", "filter", None, None),
        ),
        out_specs=(
            P("dp", "filter", None, None),
            P("dp", None, None, "filter"),
            P("dp", None, None, "filter"),
        ),
        check_vma=False,
    )
```

profile of v0, /device:TPU:1, one launch (start us, length us, event | category | flops | bytes accessed | tf_op | source)
XLA Modules:
  0.0 268.3 jit_solution(1624768555959365311)
XLA Ops:
  7.2 0.0 all-gather.2.cloned.1.call-start
  7.2 0.7 all-gather.2.cloned.1.call-update
  7.9 0.0 all-reduce.4.cloned.1.call-start
  8.0 4.1 %fusion.124 = f32[48,24,1024]{2,1,0:T(8,128)} fusion(bf16[3,3,128,1024]{3,2,1,0:T(8,128)(2,1)} %param.4, bf16[48,24,128]{2,1,0:T(8,128)(2,1)} %bitcast.236), kind=kOutput, calls=%fused_computation.79 | convolution fusion | flops 301989888 | bytes 5275648 | tf_op jit(solution)/shard_map/hwi,io->hwo/dot_general | solution.py:11
  12.0 3.8 %fusion.127 = f32[48,24,1024]{2,1,0:T(8,128)} fusion(bf16[3,3,128,1024]{3,2,1,0:T(8,128)(2,1)} %param.4, bf16[48,24,128]{2,1,0:T(8,128)(2,1)S(1)} %bitcast.237), kind=kOutput, calls=%fused_computation.82 | convolution fusion | flops 301989888 | bytes 5275648 | tf_op jit(solution)/shard_map/hwi,io->hwo/dot_general | solution.py:11
  15.8 3.9 %fusion.130 = f32[48,24,1024]{2,1,0:T(8,128)} fusion(bf16[3,3,128,1024]{3,2,1,0:T(8,128)(2,1)} %param.4, bf16[48,24,128]{2,1,0:T(8,128)(2,1)S(1)} %bitcast.238), kind=kOutput, calls=%fused_computation.85 | convolution fusion | flops 301989888 | bytes 5275648 | tf_op jit(solution)/shard_map/hwi,io->hwo/dot_general | solution.py:11
  19.8 3.9 %fusion.136 = f32[48,24,1024]{2,1,0:T(8,128)} fusion(bf16[3,3,128,1024]{3,2,1,0:T(8,128)(2,1)} %param.4, bf16[48,24,128]{2,1,0:T(8,128)(2,1)S(1)} %bitcast.239), kind=kOutput, calls=%fused_computation.91 | convolution fusion | flops 301989888 | bytes 5275648 | tf_op jit(solution)/shard_map/hwi,io->hwo/dot_general | solution.py:11
  23.6 3.9 %fusion.139 = f32[48,24,1024]{2,1,0:T(8,128)} fusion(bf16[3,3,128,1024]{3,2,1,0:T(8,128)(2,1)} %param.4, bf16[48,24,128]{2,1,0:T(8,128)(2,1)S(1)} %bitcast.240), kind=kOutput, calls=%fused_computation.94 | convolution fusion | flops 301989888 | bytes 5275648 | tf_op jit(solution)/shard_map/hwi,io->hwo/dot_general | solution.py:11
  27.5 24.7 %all-gather.2.cloned.1.call-done = bf16[1,48,24,1024]{3,2,0,1:T(8,128)(2,1)} async-done(((bf16[1,6,24,1024]{3,2,0,1:T(8,128)(2,1)}), bf16[1,48,24,1024]{3,2,0,1:T(8,128)(2,1)}) %all-gather.2.cloned.1.call-update) | async-done | bytes 2359312 | tf_op jit(solution)/shard_map/all_gather | solution.py:38
  52.3 3.2 %fusion.69 = f32[1024,9,128]{0,2,1:T(8,128)} fusion(bf16[1,48,24,1024]{3,2,0,1:T(8,128)(2,1)} %all-gather.2.cloned.1.call-done, bf16[48,24,128]{2,1,0:T(8,128)(2,1)S(1)} %bitcast.241), kind=kOutput, calls=%fused_computation.48 | convolution fusion | flops 301989888 | bytes 3178496 | tf_op jit(solution)/shard_map/hwi,hwo->oi/dot_general | solution.py:49
  55.4 1.3 fusion.75
  56.8 1.4 fusion.81
  58.1 1.4 fusion.87
  59.5 1.4 fusion.93
  60.9 1.3 fusion.99
  62.2 1.3 fusion.105
  63.5 1.4 fusion.111
  64.9 1.4 fusion.117
  66.3 6.0 %copy.46 = f32[1024,3,3,128]{3,0,2,1:T(8,128)} copy(f32[1024,3,3,128]{0,3,2,1:T(8,128)} %bitcast.58) | data formatting | bytes 9437184 | tf_op jit(solution)/shard_map/reshape | solution.py:56
  72.3 0.0 all-reduce.4.cloned.1.call-update
  72.3 0.0 reduce-scatter.2.cloned.1.call-start
  72.4 0.0 slice-start.2
  72.4 4.2 %fusion.145 = f32[48,24,1024]{2,1,0:T(8,128)} fusion(bf16[3,3,128,1024]{3,2,1,0:T(8,128)(2,1)} %param.4, bf16[48,24,128]{2,1,0:T(8,128)(2,1)S(1)} %bitcast.249), kind=kOutput, calls=%fused_computation.100 | convolution fusion | flops 301989888 | bytes 5275648 | tf_op jit(solution)/shard_map/hwi,io->hwo/dot_general | solution.py:11
  76.6 4.0 %fusion.142 = f32[48,24,1024]{2,1,0:T(8,128)} fusion(bf16[3,3,128,1024]{3,2,1,0:T(8,128)(2,1)} %param.4, bf16[48,24,128]{2,1,0:T(8,128)(2,1)S(1)} %bitcast.250), kind=kOutput, calls=%fused_computation.97 | convolution fusion | flops 301989888 | bytes 5275648 | tf_op jit(solution)/shard_map/hwi,io->hwo/dot_general | solution.py:11
  80.6 3.9 %fusion.133 = f32[48,24,1024]{2,1,0:T(8,128)} fusion(bf16[3,3,128,1024]{3,2,1,0:T(8,128)(2,1)} %param.4, bf16[1,48,24,128]{3,2,1,0:T(8,128)(2,1)S(1)} %copy-done.1), kind=kOutput, calls=%fused_computation.88 | convolution fusion | flops 301989888 | bytes 5275648 | tf_op jit(solution)/shard_map/hwi,io->hwo/dot_general | solution.py:11
  84.6 13.1 %add_add_fusion = f32[48,24,1024]{2,1,0:T(8,128)} fusion(f32[48,24,1024]{2,1,0:T(8,128)S(1)} %bitcast.253, f32[48,24,1024]{2,1,0:T(8,128)S(1)} %bitcast.255, f32[48,24,1024]{2,1,0:T(8,128)} %fusion.130, f32[48,24,1024]{2,1,0:T(8,128)} %fusion.133, f32[48,24,1024]{2,1,0:T(8,128)} %fusion.136, f32[48,24,1024]{2,1,0:T(8,128)} %fusion.139, ...), kind=kOutput, calls=%fused_computation | convolution fusion | flops 311427072 | bytes 43024384 | tf_op jit(solution)/shard_map/hwi,io->hwo/dot_general | solution.py:11
  97.7 0.0 reduce-scatter.2.cloned.1.call-update
  97.7 1.7 fusion.34
  99.5 0.1 dynamic_update_slice.27
  99.6 2.6 fusion.36
  102.1 6.3 %dynamic_update_slice.28 = f32[50,26,128]{2,1,0:T(8,128)S(1)} dynamic-update-slice(f32[50,26,128]{2,1,0:T(8,128)S(1)} %dynamic_update_slice.27, f32[48,24,128]{2,1,0:T(8,128)} %fusion.36, s32[]{:T(128)} %constant.5.clone.1, s32[]{:T(128)} %constant.6.clone.1, s32[]{:T(128)} %constant.5.clone.1) | dynamic-update-slice | bytes 1179652 | tf_op jit(solution)/shard_map/dynamic_update_slice | solution.py:47
  108.5 2.6 fusion.39
  111.0 6.3 %dynamic_update_slice.29 = f32[50,26,128]{2,1,0:T(8,128)S(1)} dynamic-update-slice(f32[50,26,128]{2,1,0:T(8,128)S(1)} %dynamic_update_slice.28, f32[48,24,128]{2,1,0:T(8,128)} %fusion.39, s32[]{:T(128)} %constant.5.clone.1, s32[]{:T(128)} %constant.7.clone.1, s32[]{:T(128)} %constant.5.clone.1) | dynamic-update-slice | bytes 1179652 | tf_op jit(solution)/shard_map/dynamic_update_slice | solution.py:47
  117.3 1.9 fusion.45
  119.2 2.6 fusion.48
  121.8 6.3 %dynamic_update_slice.31 = f32[50,26,128]{2,1,0:T(8,128)S(1)} dynamic-update-slice(f32[50,26,128]{2,1,0:T(8,128)S(1)} %fusion.45, f32[48,24,128]{2,1,0:T(8,128)} %fusion.48, s32[]{:T(128)} %constant.6.clone.1, s32[]{:T(128)} %constant.6.clone.1, s32[]{:T(128)} %constant.5.clone.1) | dynamic-update-slice | bytes 1179652 | tf_op jit(solution)/shard_map/dynamic_update_slice | solution.py:47
  128.1 2.6 fusion.51
  130.6 6.3 %dynamic_update_slice.32 = f32[50,26,128]{2,1,0:T(8,128)S(1)} dynamic-update-slice(f32[50,26,128]{2,1,0:T(8,128)S(1)} %dynamic_update_slice.31, f32[48,24,128]{2,1,0:T(8,128)} %fusion.51, s32[]{:T(128)} %constant.6.clone.1, s32[]{:T(128)} %constant.7.clone.1, s32[]{:T(128)} %constant.5.clone.1) | dynamic-update-slice | bytes 1179652 | tf_op jit(solution)/shard_map/dynamic_update_slice | solution.py:47
  136.9 1.8 fusion.57
  138.8 2.6 fusion.60
  141.3 6.2 %dynamic_update_slice.34 = f32[50,26,128]{2,1,0:T(8,128)S(1)} dynamic-update-slice(f32[50,26,128]{2,1,0:T(8,128)S(1)} %fusion.57, f32[48,24,128]{2,1,0:T(8,128)} %fusion.60, s32[]{:T(128)} %constant.7.clone.1, s32[]{:T(128)} %constant.6.clone.1, s32[]{:T(128)} %constant.5.clone.1) | dynamic-update-slice | bytes 1179652 | tf_op jit(solution)/shard_map/dynamic_update_slice | solution.py:47
  147.6 2.6 fusion.63
  150.1 6.2 %dynamic_update_slice.35 = f32[50,26,128]{2,1,0:T(8,128)S(1)} dynamic-update-slice(f32[50,26,128]{2,1,0:T(8,128)S(1)} %dynamic_update_slice.34, f32[48,24,128]{2,1,0:T(8,128)} %fusion.63, s32[]{:T(128)} %constant.7.clone.1, s32[]{:T(128)} %constant.7.clone.1, s32[]{:T(128)} %constant.5.clone.1) | dynamic-update-slice | bytes 1179652 | tf_op jit(solution)/shard_map/dynamic_update_slice | solution.py:47
  156.4 0.8 fusion.120
  157.1 40.0 %all-reduce.4.cloned.1.call-done = f32[1024,3,3,128]{3,0,2,1:T(8,128)} async-done(((f32[1024,3,3,128]{3,0,2,1:T(8,128)}), f32[1024,3,3,128]{3,0,2,1:T(8,128)}) %all-reduce.4.cloned.1.call-update) | async-done | bytes 4718608 | tf_op jit(solution)/shard_map/psum | solution.py:61
  197.2 1.6 dynamic-slice_multiply_fusion
  198.8 61.2 %reduce-scatter.2.cloned.1.call-done = f32[6,24,1024]{2,1,0:T(8,128)} async-done(((f32[48,24,1024]{2,1,0:T(8,128)}), f32[6,24,1024]{2,1,0:T(8,128)}) %reduce-scatter.2.cloned.1.call-update) | async-done | bytes 589840 | tf_op jit(solution)/shard_map/reduce_scatter | solution.py:29
  259.9 1.8 convert_bitcast_fusion
  (13 shorter events, 0.0 us)
Async XLA Ops:
  7.2 45.1 %all-gather.2.cloned.1.call-start = ((), (), s32[]{:S(2)}) async-start(), calls=%async_computation.2 | async-start | bytes 2654208 | tf_op jit(solution)/shard_map/all_gather | solution.py:38
  7.9 189.3 %all-reduce.4.cloned.1.call-start = ((), (), s32[]{:S(2)}) async-start(), calls=%async_computation.3 | async-start | bytes 9437184 | tf_op jit(solution)/shard_map/psum | solution.py:61
  7.9 4.1 %copy-start.1 = (bf16[1,48,24,128]{3,2,1,0:T(8,128)(2,1)S(1)}, bf16[1,48,24,128]{3,2,1,0:T(8,128)(2,1)}, u32[]{:S(2)}) copy-start(bf16[1,48,24,128]{3,2,1,0:T(8,128)(2,1)} %param.3) | copy-start | bytes 884740
  52.3 3.2 %copy-start = (bf16[1,48,24,1024]{3,2,0,1:T(8,128)(2,1)S(1)}, bf16[1,48,24,1024]{3,2,0,1:T(8,128)(2,1)}, u32[]{:S(2)}) copy-start(bf16[1,48,24,1024]{3,2,0,1:T(8,128)(2,1)} %all-gather.2.cloned.1.call-done) | copy-start | bytes 7077892
  72.3 187.6 %reduce-scatter.2.cloned.1.call-start = ((), (), s32[]{:S(2)}) async-start(), calls=%async_computation.1 | async-start | bytes 5308416 | tf_op jit(solution)/shard_map/reduce_scatter | solution.py:29
  72.4 12.2 %slice-start = ((s8[4718592]{0:T(1024)(128)(4,1)}), s8[4194304]{0:T(1024)(128)(4,1)S(1)}, s32[]{:S(2)}) async-start(s8[4718592]{0:T(1024)(128)(4,1)} %bitcast.252), calls=%async_computation.4 | async-start | bytes 8388608
  72.4 12.2 %slice-start.2 = ((s8[4718592]{0:T(1024)(128)(4,1)}), s8[4194304]{0:T(1024)(128)(4,1)S(1)}, s32[]{:S(2)}) async-start(s8[4718592]{0:T(1024)(128)(4,1)} %bitcast.254), calls=%async_computation.6 | async-start | bytes 8388608
  76.6 8.0 %slice-start.1 = ((s8[4718592]{0:T(1024)(128)(4,1)}), s8[524288]{0:T(1024)(128)(4,1)S(1)}, s32[]{:S(2)}) async-start(s8[4718592]{0:T(1024)(128)(4,1)} %bitcast.252), calls=%async_computation.5 | async-start | bytes 1048576
  76.6 8.0 %slice-start.3 = ((s8[4718592]{0:T(1024)(128)(4,1)}), s8[524288]{0:T(1024)(128)(4,1)S(1)}, s32[]{:S(2)}) async-start(s8[4718592]{0:T(1024)(128)(4,1)} %bitcast.254), calls=%async_computation.7 | async-start | bytes 1048576
Sparse Core Ops, SparseCore 0:
  9.8 42.4 all-gather.1
  72.5 124.6 all-reduce.3
  199.9 59.9 reduce-scatter.1
where the time goes:
time: 270 us; the launch traced here: 268 us
  waiting for transfers between devices  127 us (47%)
  matrix products  79.7 us (30%)
  local copies, waits for them, and re-layouts  44.6 us (17%)
  between operations  13.9 us (5%)
  other arithmetic  3.4 us (1%)
    reduce_scatter x1, waiting for transfers between devices, on_device(): lax.psum_scatter(conv_rows(xpad, kernel, my_rows * lax.axis_size('filter'...  61.2 us
    dot_general x9, matrix products, conv_rows(): jnp.einsum('hwi,io->hwo', xpad[a:a + count, b:b + width], weights[a, b],...  44.8 us
    psum x1, waiting for transfers between devices, on_device(): whole = lax.psum(grads, 'dp')  40 us
    dynamic_update_slice x7, local copies, waits for them, and re-layouts, on_device(): lax.dynamic_update_slice(back_pad, region + contrib, (start + a, b, 0))  37.7 us
    all_gather x1, waiting for transfers between devices, on_device(): grad_rows = lax.all_gather(cotangent, 'filter', axis=1, tiled=True)[0]  24.7 us
    dot_general x9, matrix products, on_device(): jnp.einsum('hwo,io->hwi', grad_rows, kernel[a, b], preferred_element_type...  20.9 us
    dot_general x9, matrix products, on_device(): jnp.einsum('hwi,hwo->oi', xpad[a:a + count, b:b + width], grad_rows, pref...  14 us
    reshape x1, local copies, waits for them, and re-layouts, on_device(): grads = jnp.stack(taps, 1).reshape(channels, 3, 3, local_in)  6.04 us
  transfers between devices with their start and end apart: 3, of which 3 were waited for; matrix products, arithmetic and copies ran while one was open for 39% of the time, Pallas kernels for 0%

commit v1 on v0

--- a/solution.py
+++ b/solution.py
@@ -2,6 +2,22 @@
 import jax.numpy as jnp
 from jax import lax
 from jax.sharding import PartitionSpec as P
+
+
+def collect(x, axis, dim):
+    ways, here, step = (lax.axis_size(axis), lax.axis_index(axis), x.shape[dim])
+    shape = [n * ways if d == dim else n for d, n in enumerate(x.shape)]
+    full = lax.dynamic_update_slice_in_dim(jnp.zeros(shape, x.dtype), x, here * step, axis=dim)
+    going_up = going_down = x
+    for far in range(1, ways // 2 + 1):
+        going_up = lax.ppermute(going_up, axis, [(d, (d + 1) % ways) for d in range(ways)])
+        full = lax.dynamic_update_slice_in_dim(full, going_up, (here - far) % ways * step, axis=dim)
+        if 2 * far < ways:
+            going_down = lax.ppermute(going_down, axis, [(d, (d - 1) % ways) for d in range(ways)])
+            full = lax.dynamic_update_slice_in_dim(
+                full, going_down, (here + far) % ways * step, axis=dim
+            )
+    return full
 
 
 def conv_rows(xpad, weights, count, width):
@@ -35,7 +51,7 @@
     outputs = summed.astype(jnp.bfloat16)[None]
     start = jnp.int32(0)
     back_pad = jnp.zeros((height + 2, width + 2, local_in), jnp.float32)
-    grad_rows = lax.all_gather(cotangent, "filter", axis=1, tiled=True)[0]
+    grad_rows = collect(cotangent, "filter", 1)[0]
     count = grad_rows.shape[0]
     taps = []
     for a in range(3):

time: 270 us -> 222 us (0.82)
  waiting for transfers between devices: 127 us -> 44.2 us
  local copies, waits for them, and re-layouts: 44.6 us -> 62.5 us
  starting transfers between devices: 0.12 us -> 11.9 us
  other arithmetic: 3.4 us -> 9.46 us
  matrix products: 79.7 us -> 76.1 us
    reduce_scatter x1, waiting for transfers between devices: 61.2 us -> 0.01 us  [on_device(): lax.psum_scatter(conv_rows(xpad, kernel, my_rows * lax.axis_size('filter'...]
    all_gather x1 -> x0, waiting for transfers between devices: 24.7 us -> none  [on_device(): grad_rows = lax.all_gather(cotangent, 'filter', axis=1, tiled=True)[0]]
    dynamic_update_slice x0 -> x8, local copies, waits for them, and re-layouts: none -> 12 us  [the longest x4 5.94 us: collect(): lax.dynamic_update_slice_in_dim(full, going_up, (here - far) % ways * ste...]
    ppermute x0 -> x7, starting transfers between devices: none -> 11.8 us  [the longest x3 9.27 us: collect(): lax.ppermute(going_down, axis, [(d, (d - 1) % ways) for d in range(ways)])]
    squeeze x0 -> x9, local copies, waits for them, and re-layouts: none -> 8.38 us  [on_device(): grad_rows = collect(cotangent, 'filter', 1)[0]]
    reshape x1 -> x0, local copies, waits for them, and re-layouts: 6.04 us -> none  [on_device(): grads = jnp.stack(taps, 1).reshape(channels, 3, 3, local_in)]
    add x0 -> x6, other arithmetic: none -> 5.5 us  [on_device(): region + contrib]
    dot_general x9, matrix products: 20.9 us -> 15.6 us  [on_device(): jnp.einsum('hwo,io->hwi', grad_rows, kernel[a, b], preferred_element_type...]
  transfers between devices with their start and end apart: 3 -> 9, of which waited for: 3 -> 3; matrix products, arithmetic and copies ran while one was open for 39% -> 58% of each run, Pallas kernels for 0% -> 0%
where the time goes in v1:
time: 222 us; the launch traced here: 220 us
  matrix products  76.1 us (34%)
  local copies, waits for them, and re-layouts  62.5 us (28%)
  waiting for transfers between devices  44.2 us (20%)
  between operations  15.9 us (7%)
  starting transfers between devices  11.9 us (5%)
  other arithmetic  9.46 us (4%)
    dot_general x9, matrix products, conv_rows(): jnp.einsum('hwi,io->hwo', xpad[a:a + count, b:b + width], weights[a, b],...  45 us
    psum x1, waiting for transfers between devices, on_device(): whole = lax.psum(grads, 'dp')  40.4 us
    dynamic_update_slice x7, local copies, waits for them, and re-layouts, on_device(): lax.dynamic_update_slice(back_pad, region + contrib, (start + a, b, 0))  37 us
    dot_general x9, matrix products, on_device(): jnp.einsum('hwo,io->hwi', grad_rows, kernel[a, b], preferred_element_type...  15.6 us
    dot_general x9, matrix products, on_device(): jnp.einsum('hwi,hwo->oi', xpad[a:a + count, b:b + width], grad_rows, pref...  15.5 us
    ppermute x3, starting transfers between devices, collect(): lax.ppermute(going_down, axis, [(d, (d - 1) % ways) for d in range(ways)])  9.27 us
    squeeze x9, local copies, waits for them, and re-layouts, on_device(): grad_rows = collect(cotangent, 'filter', 1)[0]  8.38 us
    dynamic_update_slice x4, local copies, waits for them, and re-layouts, collect(): lax.dynamic_update_slice_in_dim(full, going_up, (here - far) % ways * ste...  5.94 us
  transfers between devices with their start and end apart: 9, of which 3 were waited for; matrix products, arithmetic and copies ran while one was open for 58% of the time, Pallas kernels for 0%

profile of v1, /device:TPU:1, one launch (start us, length us, event | category | flops | bytes accessed | tf_op | source)
XLA Modules:
  0.0 220.0 jit_solution(7705846912188126676)
XLA Ops:
  8.1 2.5 %collective-permute-start = (bf16[1,6,24,1024]{3,2,1,0:T(8,128)(2,1)}, bf16[1,6,24,1024]{3,2,1,0:T(8,128)(2,1)}, u32[]{:S(2)}, u32[]{:S(2)}) collective-permute-start(bf16[1,6,24,1024]{3,2,1,0:T(8,128)(2,1)} %param.5), channel_id=1, source_target_pairs={{0,1},{1,2},{2,3},{3,4},{4,5},{5,6},{6,7},{7,0},{8,9},{9,10},{10,1... | collective-permute-start | bytes 884744 | tf_op jit(solution)/shard_map/ppermute | solution.py:13
  10.6 4.0 %collective-permute-start.1 = (bf16[1,6,24,1024]{3,2,1,0:T(8,128)(2,1)}, bf16[1,6,24,1024]{3,2,1,0:T(8,128)(2,1)}, u32[]{:S(2)}, u32[]{:S(2)}) collective-permute-start(bf16[1,6,24,1024]{3,2,1,0:T(8,128)(2,1)} %param.5), channel_id=1, source_target_pairs={{0,7},{1,0},{2,1},{3,2},{4,3},{5,4},{6,5},{7,6},{8,15},{9,8},{10,9... | collective-permute-start | bytes 884744 | tf_op jit(solution)/shard_map/ppermute | solution.py:16
  14.6 4.1 %pad_slice_fusion = (bf16[48,24,128]{2,1,0:T(8,128)(2,1)}, bf16[48,24,128]{2,1,0:T(8,128)(2,1)}, bf16[48,24,128]{2,1,0:T(8,128)(2,1)}, bf16[48,24,128]{2,1,0:T(8...) fusion(bf16[48,24,128]{2,1,0:T(8,128)(2,1)} %bitcast.142), kind=kLoop, calls=%fused_computation.30 | loop fusion | bytes 2654208 | tf_op jit(solution)/shard_map/slice | solution.py:29
  18.7 3.9 %fusion.26 = f32[48,24,1024]{2,1,0:T(8,128)} fusion(bf16[3,3,128,1024]{3,2,1,0:T(8,128)(2,1)} %param.4, bf16[48,24,128]{2,1,0:T(8,128)(2,1)S(1)} %bitcast.143), kind=kOutput, calls=%fused_computation.54 | convolution fusion | flops 301989888 | bytes 5275648 | tf_op jit(solution)/shard_map/hwi,io->hwo/dot_general | solution.py:27
  23.1 1.5 dynamic_update_slice.59
  24.7 3.9 %fusion.30 = f32[48,24,1024]{2,1,0:T(8,128)} fusion(bf16[3,3,128,1024]{3,2,1,0:T(8,128)(2,1)} %param.4, bf16[48,24,128]{2,1,0:T(8,128)(2,1)S(1)} %bitcast.144), kind=kOutput, calls=%fused_computation.58 | convolution fusion | flops 301989888 | bytes 5275648 | tf_op jit(solution)/shard_map/hwi,io->hwo/dot_general | solution.py:27
  28.6 3.9 %fusion.34 = f32[48,24,1024]{2,1,0:T(8,128)} fusion(bf16[3,3,128,1024]{3,2,1,0:T(8,128)(2,1)} %param.4, bf16[48,24,128]{2,1,0:T(8,128)(2,1)S(1)} %bitcast.145), kind=kOutput, calls=%fused_computation.62 | convolution fusion | flops 301989888 | bytes 5275648 | tf_op jit(solution)/shard_map/hwi,io->hwo/dot_general | solution.py:27
  32.5 2.7 %collective-permute-start.3 = (bf16[1,6,24,1024]{3,2,1,0:T(8,128)(2,1)}, bf16[1,6,24,1024]{3,2,1,0:T(8,128)(2,1)}, u32[]{:S(2)}, u32[]{:S(2)}) collective-permute-start(bf16[1,6,24,1024]{3,2,1,0:T(8,128)(2,1)} %collective-permute-done.1), channel_id=1, source_target_pairs={{0,7},{1,0},{2,1},{3,2},{4,3},{5,4},{6,5},{7,6},{8,15},{9,8},{10,9... | collective-permute-start | bytes 884744 | tf_op jit(solution)/shard_map/ppermute | solution.py:16
  35.2 2.4 %collective-permute-done.2 = bf16[1,6,24,1024]{3,2,1,0:T(8,128)(2,1)S(1)} collective-permute-done((bf16[1,6,24,1024]{3,2,1,0:T(8,128)(2,1)}, bf16[1,6,24,1024]{3,2,1,0:T(8,128)(2,1)S(1)}, u32[]{:S(2)}, u32[]{:S(2)}) %collective-permute-start.2) | collective-permute-done | bytes 294944 | tf_op jit(solution)/shard_map/ppermute | solution.py:13
  37.6 3.9 %fusion.42 = f32[48,24,1024]{2,1,0:T(8,128)} fusion(bf16[3,3,128,1024]{3,2,1,0:T(8,128)(2,1)} %param.4, bf16[48,24,128]{2,1,0:T(8,128)(2,1)S(1)} %bitcast.146), kind=kOutput, calls=%fused_computation.70 | convolution fusion | flops 301989888 | bytes 5275648 | tf_op jit(solution)/shard_map/hwi,io->hwo/dot_general | solution.py:27
  41.5 2.6 %collective-permute-start.5 = (bf16[1,6,24,1024]{3,2,1,0:T(8,128)(2,1)}, bf16[1,6,24,1024]{3,2,1,0:T(8,128)(2,1)}, u32[]{:S(2)}, u32[]{:S(2)}) collective-permute-start(bf16[1,6,24,1024]{3,2,1,0:T(8,128)(2,1)} %collective-permute-done.3), channel_id=1, source_target_pairs={{0,7},{1,0},{2,1},{3,2},{4,3},{5,4},{6,5},{7,6},{8,15},{9,8},{10,9... | collective-permute-start | bytes 884744 | tf_op jit(solution)/shard_map/ppermute | solution.py:16
  45.5 3.9 %fusion.46 = f32[48,24,1024]{2,1,0:T(8,128)} fusion(bf16[3,3,128,1024]{3,2,1,0:T(8,128)(2,1)} %param.4, bf16[48,24,128]{2,1,0:T(8,128)(2,1)S(1)} %bitcast.147), kind=kOutput, calls=%fused_computation.74 | convolution fusion | flops 301989888 | bytes 5275648 | tf_op jit(solution)/shard_map/hwi,io->hwo/dot_general | solution.py:27
  53.1 1.5 dynamic_update_slice.61
  56.9 1.5 dynamic_update_slice.62
  58.4 1.5 dynamic_update_slice.63
  62.2 1.5 dynamic_update_slice.64
  66.4 1.5 dynamic_update_slice.66
  68.0 2.6 %fusion.8 = f32[1024,9,128]{2,0,1:T(8,128)} fusion(bf16[48,24,1024]{2,0,1:T(8,128)(2,1)S(1)} %dynamic_update_slice.66, bf16[48,24,128]{2,1,0:T(8,128)(2,1)} %get-tuple-element.10), kind=kOutput, calls=%fused_computation.18 | convolution fusion | flops 301989888 | bytes 3178496 | tf_op jit(solution)/shard_map/hwi,hwo->oi/dot_general | solution.py:65
  70.6 1.6 fusion.7
  72.2 1.6 fusion.6
  73.9 1.6 fusion.5
  75.5 1.6 fusion.4
  77.1 1.6 fusion.3
  78.7 1.6 fusion.2
  80.3 1.6 fusion.1
  81.9 1.6 fusion
  83.6 4.2 %fusion.54 = f32[48,24,1024]{2,1,0:T(8,128)} fusion(bf16[3,3,128,1024]{3,2,1,0:T(8,128)(2,1)} %param.4, bf16[48,24,128]{2,1,0:T(8,128)(2,1)S(1)} %bitcast.149), kind=kOutput, calls=%fused_computation.82 | convolution fusion | flops 301989888 | bytes 5275648 | tf_op jit(solution)/shard_map/hwi,io->hwo/dot_general | solution.py:27
  87.9 3.9 %fusion.50 = f32[48,24,1024]{2,1,0:T(8,128)} fusion(bf16[3,3,128,1024]{3,2,1,0:T(8,128)(2,1)} %param.4, bf16[48,24,128]{2,1,0:T(8,128)(2,1)S(1)} %bitcast.150), kind=kOutput, calls=%fused_computation.78 | convolution fusion | flops 301989888 | bytes 5275648 | tf_op jit(solution)/shard_map/hwi,io->hwo/dot_general | solution.py:27
  91.8 3.8 %fusion.38 = f32[48,24,1024]{2,1,0:T(8,128)} fusion(bf16[3,3,128,1024]{3,2,1,0:T(8,128)(2,1)} %param.4, bf16[1,48,24,128]{3,2,1,0:T(8,128)(2,1)S(1)} %copy-done), kind=kOutput, calls=%fused_computation.66 | convolution fusion | flops 301989888 | bytes 5275648 | tf_op jit(solution)/shard_map/hwi,io->hwo/dot_general | solution.py:27
  95.7 13.4 %add_add_fusion = f32[48,24,1024]{2,1,0:T(8,128)} fusion(f32[48,24,1024]{2,1,0:T(8,128)S(1)} %bitcast.153, f32[48,24,1024]{2,1,0:T(8,128)S(1)} %bitcast.155, f32[48,24,1024]{2,1,0:T(8,128)} %fusion.34, f32[48,24,1024]{2,1,0:T(8,128)} %fusion.38, f32[48,24,1024]{2,1,0:T(8,128)} %fusion.42, f32[48,24,1024]{2,1,0:T(8,128)} %fusion.46, ...), kind=kOutput, calls=%fused_computation | convolution fusion | flops 311427072 | bytes 43024384 | tf_op jit(solution)/shard_map/hwi,io->hwo/dot_general | solution.py:27
  109.1 1.7 fusion.52
  111.2 1.7 fusion.48
  113.9 6.3 %dynamic_update_slice.68 = f32[50,26,128]{2,1,0:T(8,128)S(1)} dynamic-update-slice(f32[50,26,128]{2,1,0:T(8,128)S(1)} %dynamic_update_slice.67, f32[48,24,128]{2,1,0:T(8,128)} %copy_add_fusion, s32[]{:T(128)} %constant.68.clone.1, s32[]{:T(128)} %constant.73.clone.1, s32[]{:T(128)} %constant.68.clone.1) | dynamic-update-slice | bytes 1179652 | tf_op jit(solution)/shard_map/dynamic_update_slice | solution.py:63
  120.3 1.7 fusion.44
  123.0 6.3 %dynamic_update_slice.69 = f32[50,26,128]{2,1,0:T(8,128)S(1)} dynamic-update-slice(f32[50,26,128]{2,1,0:T(8,128)S(1)} %dynamic_update_slice.68, f32[48,24,128]{2,1,0:T(8,128)} %slice_add_fusion.6, s32[]{:T(128)} %constant.68.clone.1, s32[]{:T(128)} %constant.75.clone.1, s32[]{:T(128)} %constant.68.clone.1) | dynamic-update-slice | bytes 1179652 | tf_op jit(solution)/shard_map/dynamic_update_slice | solution.py:63
  129.4 1.7 fusion.40
  131.4 1.7 fusion.36
  134.2 6.3 %dynamic_update_slice.71 = f32[50,26,128]{2,1,0:T(8,128)S(1)} dynamic-update-slice(f32[50,26,128]{2,1,0:T(8,128)S(1)} %fusion.10, f32[48,24,128]{2,1,0:T(8,128)} %slice_add_fusion.4, s32[]{:T(128)} %constant.73.clone.1, s32[]{:T(128)} %constant.73.clone.1, s32[]{:T(128)} %constant.68.clone.1) | dynamic-update-slice | bytes 1179652 | tf_op jit(solution)/shard_map/dynamic_update_slice | solution.py:63
  140.4 1.7 fusion.32
  143.2 6.3 %dynamic_update_slice.72 = f32[50,26,128]{2,1,0:T(8,128)S(1)} dynamic-update-slice(f32[50,26,128]{2,1,0:T(8,128)S(1)} %dynamic_update_slice.71, f32[48,24,128]{2,1,0:T(8,128)} %slice_add_fusion.3, s32[]{:T(128)} %constant.73.clone.1, s32[]{:T(128)} %constant.75.clone.1, s32[]{:T(128)} %constant.68.clone.1) | dynamic-update-slice | bytes 1179652 | tf_op jit(solution)/shard_map/dynamic_update_slice | solution.py:63
  149.5 1.7 fusion.28
  151.5 1.7 fusion.24
  154.3 6.2 %dynamic_update_slice.74 = f32[50,26,128]{2,1,0:T(8,128)S(1)} dynamic-update-slice(f32[50,26,128]{2,1,0:T(8,128)S(1)} %fusion.9, f32[48,24,128]{2,1,0:T(8,128)} %slice_add_fusion.1, s32[]{:T(128)} %constant.75.clone.1, s32[]{:T(128)} %constant.73.clone.1, s32[]{:T(128)} %constant.68.clone.1) | dynamic-update-slice | bytes 1179652 | tf_op jit(solution)/shard_map/dynamic_update_slice | solution.py:63
  160.5 1.7 fusion.21
  162.5 5.5 %dynamic_update_slice.75 = f32[50,26,128]{2,1,0:T(8,128)S(1)} dynamic-update-slice(f32[50,26,128]{2,1,0:T(8,128)S(1)} %dynamic_update_slice.74, f32[48,24,128]{2,1,0:T(8,128)S(1)} %slice_add_fusion, s32[]{:T(128)} %constant.75.clone.1, s32[]{:T(128)} %constant.75.clone.1, s32[]{:T(128)} %constant.68.clone.1) | dynamic-update-slice | bytes 1179652 | tf_op jit(solution)/shard_map/dynamic_update_slice | solution.py:63
  168.8 40.4 %all-reduce.4.cloned.1.call-done = f32[1024,3,3,128]{3,0,2,1:T(8,128)} async-done(((f32[1024,3,3,128]{3,0,2,1:T(8,128)}), f32[1024,3,3,128]{3,0,2,1:T(8,128)}) %all-reduce.4.cloned.1.call-update) | async-done | bytes 4718608 | tf_op jit(solution)/shard_map/psum | solution.py:77
  209.2 1.6 dynamic-slice_multiply_fusion
  210.8 1.8 convert_bitcast_fusion
  (66 shorter events, 20.0 us)
Async XLA Ops:
  8.0 10.7 %copy-start = (bf16[1,48,24,128]{3,2,1,0:T(8,128)(2,1)S(1)}, bf16[1,48,24,128]{3,2,1,0:T(8,128)(2,1)}, u32[]{:S(2)}) copy-start(bf16[1,48,24,128]{3,2,1,0:T(8,128)(2,1)} %param.3) | copy-start | bytes 884740
  8.0 201.2 %all-reduce.4.cloned.1.call-start = ((), (), s32[]{:S(2)}) async-start(), calls=%async_computation.2 | async-start | bytes 9437184 | tf_op jit(solution)/shard_map/psum | solution.py:77
  8.1 20.5 %collective-permute-start = (bf16[1,6,24,1024]{3,2,1,0:T(8,128)(2,1)}, bf16[1,6,24,1024]{3,2,1,0:T(8,128)(2,1)}, u32[]{:S(2)}, u32[]{:S(2)}) collective-permute-start(bf16[1,6,24,1024]{3,2,1,0:T(8,128)(2,1)} %param.5), channel_id=1, source_target_pairs={{0,1},{1,2},{2,3},{3,4},{4,5},{5,6},{6,7},{7,0},{8,9},{9,10},{10,1... | collective-permute-start | bytes 884744 | tf_op jit(solution)/shard_map/ppermute | solution.py:13
  10.6 21.9 %collective-permute-start.1 = (bf16[1,6,24,1024]{3,2,1,0:T(8,128)(2,1)}, bf16[1,6,24,1024]{3,2,1,0:T(8,128)(2,1)}, u32[]{:S(2)}, u32[]{:S(2)}) collective-permute-start(bf16[1,6,24,1024]{3,2,1,0:T(8,128)(2,1)} %param.5), channel_id=1, source_target_pairs={{0,7},{1,0},{2,1},{3,2},{4,3},{5,4},{6,5},{7,6},{8,15},{9,8},{10,9... | collective-permute-start | bytes 884744 | tf_op jit(solution)/shard_map/ppermute | solution.py:16
  18.7 3.9 %copy-start.1 = (bf16[1,6,24,1024]{3,2,1,0:T(8,128)(2,1)S(1)}, bf16[1,6,24,1024]{3,2,1,0:T(8,128)(2,1)}, u32[]{:S(2)}) copy-start(bf16[1,6,24,1024]{3,2,1,0:T(8,128)(2,1)} %param.5) | copy-start | bytes 884740
  28.6 9.0 %collective-permute-start.2 = (bf16[1,6,24,1024]{3,2,1,0:T(8,128)(2,1)}, bf16[1,6,24,1024]{3,2,1,0:T(8,128)(2,1)S(1)}, u32[]{:S(2)}, u32[]{:S(2)}) collective-permute-start(bf16[1,6,24,1024]{3,2,1,0:T(8,128)(2,1)} %collective-permute-done), channel_id=1, source_target_pairs={{0,1},{1,2},{2,3},{3,4},{4,5},{5,6},{6,7},{7,0},{8,9},{9,10},{10,1... | collective-permute-start | bytes 884744 | tf_op jit(solution)/shard_map/ppermute | solution.py:13
  32.5 9.0 %collective-permute-start.3 = (bf16[1,6,24,1024]{3,2,1,0:T(8,128)(2,1)}, bf16[1,6,24,1024]{3,2,1,0:T(8,128)(2,1)}, u32[]{:S(2)}, u32[]{:S(2)}) collective-permute-start(bf16[1,6,24,1024]{3,2,1,0:T(8,128)(2,1)} %collective-permute-done.1), channel_id=1, source_target_pairs={{0,7},{1,0},{2,1},{3,2},{4,3},{5,4},{6,5},{7,6},{8,15},{9,8},{10,9... | collective-permute-start | bytes 884744 | tf_op jit(solution)/shard_map/ppermute | solution.py:16
  37.6 3.9 %copy-start.9 = (bf16[1,6,24,1024]{3,2,1,0:T(8,128)(2,1)}, bf16[1,6,24,1024]{3,2,1,0:T(8,128)(2,1)S(1)}, u32[]{:S(2)}) copy-start(bf16[1,6,24,1024]{3,2,1,0:T(8,128)(2,1)S(1)} %collective-permute-done.2) | copy-start | bytes 884740
  37.6 8.0 %collective-permute-start.4 = (bf16[1,6,24,1024]{3,2,1,0:T(8,128)(2,1)S(1)}, bf16[1,6,24,1024]{3,2,1,0:T(8,128)(2,1)}, u32[]{:S(2)}, u32[]{:S(2)}) collective-permute-start(bf16[1,6,24,1024]{3,2,1,0:T(8,128)(2,1)S(1)} %collective-permute-done.2), channel_id=1, source_target_pairs={{0,1},{1,2},{2,3},{3,4},{4,5},{5,6},{6,7},{7,0},{8,9},{9,10},{10,1... | collective-permute-start | bytes 884744 | tf_op jit(solution)/shard_map/ppermute | solution.py:13
  41.5 19.6 %collective-permute-start.5 = (bf16[1,6,24,1024]{3,2,1,0:T(8,128)(2,1)}, bf16[1,6,24,1024]{3,2,1,0:T(8,128)(2,1)}, u32[]{:S(2)}, u32[]{:S(2)}) collective-permute-start(bf16[1,6,24,1024]{3,2,1,0:T(8,128)(2,1)} %collective-permute-done.3), channel_id=1, source_target_pairs={{0,7},{1,0},{2,1},{3,2},{4,3},{5,4},{6,5},{7,6},{8,15},{9,8},{10,9... | collective-permute-start | bytes 884744 | tf_op jit(solution)/shard_map/ppermute | solution.py:16
  45.5 19.8 %collective-permute-start.6 = (bf16[1,6,24,1024]{3,2,1,0:T(8,128)(2,1)}, bf16[1,6,24,1024]{3,2,1,0:T(8,128)(2,1)}, u32[]{:S(2)}, u32[]{:S(2)}) collective-permute-start(bf16[1,6,24,1024]{3,2,1,0:T(8,128)(2,1)} %collective-permute-done.4), channel_id=1, source_target_pairs={{0,1},{1,2},{2,3},{3,4},{4,5},{5,6},{6,7},{7,0},{8,9},{9,10},{10,1... | collective-permute-start | bytes 884744 | tf_op jit(solution)/shard_map/ppermute | solution.py:13
  68.0 2.6 %copy-start.8 = (bf16[48,24,128]{2,1,0:T(8,128)(2,1)S(1)}, bf16[48,24,128]{2,1,0:T(8,128)(2,1)}, u32[]{:S(2)}) copy-start(bf16[48,24,128]{2,1,0:T(8,128)(2,1)} %get-tuple-element.9) | copy-start | bytes 884740
  70.6 1.6 copy-start.7
  72.2 1.6 copy-start.6
  75.5 1.6 copy-start.5
  77.1 1.6 copy-start.4
  78.7 1.6 copy-start.3
  80.3 1.6 copy-start.2
  83.6 127.2 %reduce-scatter.2.cloned.1.call-start = ((), (), s32[]{:S(2)}) async-start(), calls=%async_computation.1 | async-start | bytes 5308416 | tf_op jit(solution)/shard_map/reduce_scatter | solution.py:45
  83.6 12.0 %slice-start = ((s8[4718592]{0:T(1024)(128)(4,1)}), s8[4194304]{0:T(1024)(128)(4,1)S(1)}, s32[]{:S(2)}) async-start(s8[4718592]{0:T(1024)(128)(4,1)} %bitcast.152), calls=%async_computation.3 | async-start | bytes 8388608
  83.6 12.0 %slice-start.2 = ((s8[4718592]{0:T(1024)(128)(4,1)}), s8[4194304]{0:T(1024)(128)(4,1)S(1)}, s32[]{:S(2)}) async-start(s8[4718592]{0:T(1024)(128)(4,1)} %bitcast.154), calls=%async_computation.5 | async-start | bytes 8388608
  87.8 7.8 %slice-start.1 = ((s8[4718592]{0:T(1024)(128)(4,1)}), s8[524288]{0:T(1024)(128)(4,1)S(1)}, s32[]{:S(2)}) async-start(s8[4718592]{0:T(1024)(128)(4,1)} %bitcast.152), calls=%async_computation.4 | async-start | bytes 1048576
  87.9 7.8 %slice-start.3 = ((s8[4718592]{0:T(1024)(128)(4,1)}), s8[524288]{0:T(1024)(128)(4,1)S(1)}, s32[]{:S(2)}) async-start(s8[4718592]{0:T(1024)(128)(4,1)} %bitcast.154), calls=%async_computation.6 | async-start | bytes 1048576
Sparse Core Ops, SparseCore 0:
  83.7 125.4 all-reduce.3
Sparse Core Ops, SparseCore 1:
  109.2 62.4 reduce-scatter.1
